TPU v7x, 512 devices: a whole 4x4x16 slice. The times are simulated.
512 devices in a mesh: ep: 64 (over z, y), dp: 8 (over x, core).
Axes of the slice: x: 4, y: 4, z: 16, core: 2. Of those that a mesh axis runs over, the one named last changes fastest.
Arguments:
- tokens: bfloat16 [12288, 3584], P(('ep', 'dp')), may hold values from -6 to 6
- grad_out: bfloat16 [12288, 3584], P(('ep', 'dp')), may hold values from -0.29882812 to 0.29882812
- routes: int32 [12288, 2], P(('ep', 'dp')), may hold values from 0 to 7, all different within a row; in each aligned block of 24 rows (0 to 23, 24 to 47, ...) at most 8 rows name the same one
- route_probs: float32 [12288, 2], P(('ep', 'dp')), may hold values from 0.1 to 1
- gate_weight: bfloat16 [64, 3584, 128], P('ep', 'dp'), may hold values from -0.09375 to 0.09375
- up_weight: bfloat16 [64, 3584, 128], P('ep', 'dp'), may hold values from -0.09375 to 0.09375
- down_weight: bfloat16 [64, 3584, 128], P('ep', 'dp'), may hold values from -0.1875 to 0.1875
Outputs:
- grad_tokens: bfloat16 [12288, 3584], P(('ep', 'dp'))
- grad_probs: float32 [12288, 2], P(('ep', 'dp'))
- grad_gate: bfloat16 [64, 3584, 128], P('ep', 'dp')
- grad_up: bfloat16 [64, 3584, 128], P('ep', 'dp')
- grad_down: bfloat16 [64, 3584, 128], P('ep', 'dp')
Inputs may be any that keep to these rules, and one draw needn't show every extreme that they name: `routes`: each row names 2 different experts. Within each aligned block of 24 rows (the tokens of one device) no expert is named by more than 8 rows; in some blocks one expert is named by exactly 8 rows.
All inputs are finite; a program needn't handle non-finite values.
Results may differ from a plain program's by a relative error of at most 0.017.
Values may be sent and summed in bfloat16 or wider, within the bound.
No kernel may reach another device: no remote copies, remote signals or barrier semaphores. Data moves between devices by JAX's collectives and lax.ppermute only.
A program may use at most 64 MiB of HBM per device.

v0:
```python
import jax
import jax.numpy as jnp
from jax import lax
from jax.sharding import PartitionSpec as P

GROUP = 8
TOP = 2
CONTRACT_HIDDEN = (((1,), (1,)), ((), ()))
CONTRACT_ROWS = (((0,), (0,)), ((), ()))


def slot_layout(routes, experts, capacity):
    flat_routes = routes.reshape(-1)
    copies = flat_routes.shape[0]
    onehot = (flat_routes[:, None] == jnp.arange(experts, dtype=jnp.int32)[None, :]).astype(
        jnp.int32
    )
    earlier = jnp.cumsum(onehot, axis=0) - onehot
    slot_rank = jnp.sum(earlier * onehot, axis=1)
    slot_index = flat_routes * capacity + slot_rank
    slot_copy = jnp.full((experts * capacity,), copies, jnp.int32)
    slot_copy = slot_copy.at[slot_index].set(jnp.arange(copies, dtype=jnp.int32))
    return (slot_index, slot_copy)


def per_device(tokens, grad_out, routes, route_probs, gate_weight, up_weight, down_weight):
    tok_count, features = tokens.shape
    ep_size = lax.axis_size("ep")
    experts = ep_size // GROUP
    slots = min(
        tok_count // GROUP,
        max(1, (4 * TOP * tok_count + 3 * experts * GROUP - 1) // (3 * experts * GROUP)),
    )
    capacity = GROUP * slots
    copies = tok_count * TOP
    slot_index, slot_copy = slot_layout(routes, experts, capacity)
    source_row = jnp.where(slot_copy < copies, slot_copy // TOP, tok_count)
    blank = jnp.zeros((1, features), jnp.bfloat16)
    send_tokens = jnp.concatenate([tokens, blank], axis=0)[source_row]
    send_grads = jnp.concatenate([grad_out, blank], axis=0)[source_row]
    flat_probs = jnp.concatenate([route_probs.reshape(-1), jnp.zeros((1,), jnp.float32)])
    send_probs = flat_probs[slot_copy]
    spread_tokens = jnp.broadcast_to(
        send_tokens.reshape(experts, 1, capacity, features), (experts, GROUP, capacity, features)
    ).reshape(ep_size, capacity, features)
    spread_grads = jnp.broadcast_to(
        send_grads.reshape(experts, 1, capacity, features), (experts, GROUP, capacity, features)
    ).reshape(ep_size, capacity, features)
    spread_probs = jnp.broadcast_to(
        send_probs.reshape(experts, 1, capacity), (experts, GROUP, capacity)
    ).reshape(ep_size, capacity)
    rows_tok, rows_grd, rows_prb = (
        lax.all_to_all(spread_tokens, "ep", split_axis=0, concat_axis=0, tiled=True),
        lax.all_to_all(spread_grads, "ep", split_axis=0, concat_axis=0, tiled=True),
        lax.all_to_all(
            spread_probs.astype(jnp.bfloat16), "ep", split_axis=0, concat_axis=0, tiled=True
        ).astype(spread_probs.dtype),
    )
    rows_in = rows_tok.reshape(-1, features)
    rows_grad = rows_grd.reshape(-1, features)
    rows_prob = rows_prb.reshape(-1)
    gate_all, up_all, down_all = (
        lax.all_gather(gate_weight, "dp", axis=1, tiled=True),
        lax.all_gather(up_weight, "dp", axis=1, tiled=True),
        lax.all_gather(down_weight, "dp", axis=1, tiled=True),
    )
    gate_full = gate_all[0]
    up_full = up_all[0]
    down_full = down_all[0]
    gate_pre = jnp.dot(rows_in, gate_full, preferred_element_type=jnp.float32)
    up_pre = jnp.dot(rows_in, up_full, preferred_element_type=jnp.float32)
    sigmoid_gate = jax.nn.sigmoid(gate_pre)
    activated = gate_pre * sigmoid_gate
    hidden = (activated * up_pre).astype(jnp.bfloat16)
    scaled = (rows_prob[:, None] * rows_grad.astype(jnp.float32)).astype(jnp.bfloat16)
    down_grad = jnp.dot(rows_grad, down_full, preferred_element_type=jnp.float32)
    scores = jnp.sum(hidden.astype(jnp.float32) * down_grad, axis=1)
    hidden_grad = rows_prob[:, None] * down_grad
    gate_grad = (
        hidden_grad * up_pre * sigmoid_gate * (1.0 + gate_pre * (1.0 - sigmoid_gate))
    ).astype(jnp.bfloat16)
    up_grad = (hidden_grad * activated).astype(jnp.bfloat16)
    token_part = (
        lax.dot_general(gate_grad, gate_full, CONTRACT_HIDDEN, preferred_element_type=jnp.float32)
        + lax.dot_general(up_grad, up_full, CONTRACT_HIDDEN, preferred_element_type=jnp.float32)
    ).astype(jnp.bfloat16)
    returned, returned_scores = (
        lax.all_to_all(
            token_part.reshape(ep_size, capacity, features),
            "ep",
            split_axis=0,
            concat_axis=0,
            tiled=True,
        ),
        lax.all_to_all(
            scores.reshape(ep_size, capacity).astype(jnp.bfloat16),
            "ep",
            split_axis=0,
            concat_axis=0,
            tiled=True,
        ).astype(jnp.float32),
    )
    slot_rows = jnp.sum(
        returned.reshape(experts, GROUP, capacity, features), axis=1, dtype=jnp.float32
    ).reshape(experts * capacity, features)
    slot_scores = jnp.sum(returned_scores.reshape(experts, GROUP, capacity), axis=1).reshape(-1)
    gate_term = lax.dot_general(
        rows_in, gate_grad, CONTRACT_ROWS, preferred_element_type=jnp.float32
    )
    up_term = lax.dot_general(rows_in, up_grad, CONTRACT_ROWS, preferred_element_type=jnp.float32)
    down_term = lax.dot_general(scaled, hidden, CONTRACT_ROWS, preferred_element_type=jnp.float32)
    gate_sum, up_sum, down_sum = (
        lax.psum_scatter(
            gate_term.astype(jnp.bfloat16), "dp", scatter_dimension=0, tiled=True
        ).astype(jnp.float32),
        lax.psum_scatter(
            up_term.astype(jnp.bfloat16), "dp", scatter_dimension=0, tiled=True
        ).astype(jnp.float32),
        lax.psum_scatter(
            down_term.astype(jnp.bfloat16), "dp", scatter_dimension=0, tiled=True
        ).astype(jnp.float32),
    )
    grad_tokens = jnp.sum(slot_rows[slot_index].reshape(tok_count, TOP, features), axis=1).astype(
        jnp.bfloat16
    )
    grad_probs = slot_scores[slot_index].reshape(tok_count, TOP)
    grad_gate = gate_sum.astype(jnp.bfloat16)[None]
    grad_up = up_sum.astype(jnp.bfloat16)[None]
    grad_down = down_sum.astype(jnp.bfloat16)[None]
    return (grad_tokens, grad_probs, grad_gate, grad_up, grad_down)


def solution(mesh):
    placed = (
        P(("ep", "dp"), None),
        P(("ep", "dp"), None),
        P(("ep", "dp"), None),
        P(("ep", "dp"), None),
        P("ep", "dp", None),
        P("ep", "dp", None),
        P("ep", "dp", None),
    )
    return jax.shard_map(
        per_device,
        mesh=mesh,
        in_specs=placed,
        out_specs=(
            P(("ep", "dp"), None),
            P(("ep", "dp"), None),
            P("ep", "dp", None),
            P("ep", "dp", None),
            P("ep", "dp", None),
        ),
        check_vma=False,
    )
```

profile of v0, /device:TPU:2, one launch (start us, length us, event | category | flops | bytes accessed | tf_op | source)
XLA Modules:
  0.0 604.3 jit_solution(18068888513377550808)
XLA Ops:
  7.2 0.7 broadcast_multiply_fusion
  7.8 0.8 copy.27
  8.6 0.8 copy.25
  9.4 0.1 reshape.119
  9.5 0.1 copy.26
  9.6 0.1 mul.61
  9.7 0.1 eq.15
  9.8 0.1 fusion.18
  9.8 0.1 reduce_window_sum.11
  9.9 0.2 select_reduce_fusion
  10.1 0.7 scatter_custom_fusion
  10.9 0.1 pad_maximum_fusion
  11.0 0.8 gather_fusion
  11.7 0.1 convert_element_type.101
  11.8 0.1 copy.28
  11.9 0.1 broadcast_in_dim.45
  12.0 0.1 convert_element_type.102
  12.1 0.7 copy.29
  12.8 18.7 %all-to-all-start = ((bf16[64,1,8]{2,1,0:T(2,128)(2,1)}), bf16[64,1,8]{2,1,0:T(2,128)(2,1)S(1)}, u32[]{:S(2)}, u32[]{:S(2)}) async-start(bf16[64,1,8]{2,1,0:T(2,128)(2,1)} %copy.29), calls=%async_computation | async-start | bytes 65536 | tf_op jit(solution)/shard_map/all_to_all | solution.py:55
  31.6 0.9 concatenate.11
  32.5 0.8 gather_fusion.2
  33.3 12.8 %all-to-all-done = bf16[64,1,8]{2,1,0:T(2,128)(2,1)S(1)} async-done(((bf16[64,1,8]{2,1,0:T(2,128)(2,1)}), bf16[64,1,8]{2,1,0:T(2,128)(2,1)S(1)}, u32[]{:S(2)}, u32[]{:S(2)}) %all-to-all-start) | async-done | bytes 1056 | tf_op jit(solution)/shard_map/all_to_all | solution.py:55
  46.1 2.1 broadcast_in_dim.51
  48.2 5.7 all-to-all-start.2
  53.9 0.0 copy-done
  54.0 0.8 gather_fusion.1
  54.8 165.5 %all-to-all-done.2 = bf16[64,8,3584]{2,1,0:T(8,128)(2,1)} async-done(((bf16[64,8,3584]{2,1,0:T(8,128)(2,1)}), bf16[64,8,3584]{2,1,0:T(8,128)(2,1)}, u32[]{:S(2)}, u32[]{:S(2)}) %all-to-all-start.2) | async-done | bytes 3670048 | tf_op jit(solution)/shard_map/all_to_all | solution.py:53
  220.3 2.1 broadcast_in_dim.49
  222.4 6.2 %all-to-all-start.1 = ((bf16[64,8,3584]{2,1,0:T(8,128)(2,1)}), bf16[64,8,3584]{2,1,0:T(8,128)(2,1)}, u32[]{:S(2)}, u32[]{:S(2)}) async-start(bf16[64,8,3584]{2,1,0:T(8,128)(2,1)} %bitcast.64), calls=%async_computation.1 | async-start | bytes 7340032 | tf_op jit(solution)/shard_map/all_to_all | solution.py:54
  228.6 0.0 copy-done.1
  228.6 13.6 %all_gather.11 = bf16[1,3584,128]{2,1,0:T(8,128)(2,1)S(1)} all-gather(bf16[1,448,128]{2,1,0:T(8,128)(2,1)S(1)} %copy-done.1), channel_id=1, replica_groups=mesh['ep'=64,'dp'=8] {'dp'}, dimensions={1}, use_global_device_ids=true | all-gather | bytes 1032192 | tf_op jit(solution)/shard_map/all_gather | solution.py:63
  242.3 13.5 %all_gather.10 = bf16[1,3584,128]{2,1,0:T(8,128)(2,1)S(1)} all-gather(bf16[1,448,128]{2,1,0:T(8,128)(2,1)S(1)} %copy-done.2), channel_id=1, replica_groups=mesh['ep'=64,'dp'=8] {'dp'}, dimensions={1}, use_global_device_ids=true | all-gather | bytes 1032192 | tf_op jit(solution)/shard_map/all_gather | solution.py:64
  255.8 13.5 %all_gather.9 = bf16[1,3584,128]{2,1,0:T(8,128)(2,1)S(1)} all-gather(bf16[1,448,128]{2,1,0:T(8,128)(2,1)S(1)} %copy-done.3), channel_id=1, replica_groups=mesh['ep'=64,'dp'=8] {'dp'}, dimensions={1}, use_global_device_ids=true | all-gather | bytes 1032192 | tf_op jit(solution)/shard_map/all_gather | solution.py:65
  269.3 0.1 convert_reduce_fusion.1
  269.4 0.1 reshape.129
  269.4 3.4 fusion.3
  272.8 3.4 fusion.5
  276.2 119.3 %all-to-all-done.1 = bf16[64,8,3584]{2,1,0:T(8,128)(2,1)} async-done(((bf16[64,8,3584]{2,1,0:T(8,128)(2,1)}), bf16[64,8,3584]{2,1,0:T(8,128)(2,1)}, u32[]{:S(2)}, u32[]{:S(2)}) %all-to-all-start.1) | async-done | bytes 3670048 | tf_op jit(solution)/shard_map/all_to_all | solution.py:54
  395.5 4.1 multiply_reduce_fusion
  399.6 0.7 convert_element_type.125
  400.3 6.0 all-to-all-start.4
  406.4 1.1 fusion.11
  407.5 3.1 fusion
  410.6 10.2 %all-to-all-done.4 = bf16[64,1,8]{2,1,0:T(2,128)(2,1)S(1)} async-done(((bf16[64,1,8]{2,1,0:T(2,128)(2,1)}), bf16[64,1,8]{2,1,0:T(2,128)(2,1)S(1)}, u32[]{:S(2)}, u32[]{:S(2)}) %all-to-all-start.4) | async-done | bytes 1056 | tf_op jit(solution)/shard_map/all_to_all | solution.py:95
  420.8 5.6 all-to-all-start.3
  426.4 0.0 reduce-scatter.8.cloned.1.call-start
  426.4 0.0 copy-done.4
  426.5 4.4 convolution_convert_fusion
  430.8 0.0 reduce-scatter.8.cloned.1.call-update
  430.9 0.0 reduce-scatter.6.cloned.1.call-start
  430.9 4.1 convolution_convert_fusion.1
  435.1 0.0 reduce-scatter.6.cloned.1.call-update
  435.1 0.0 reduce-scatter.4.cloned.1.call-start
  435.1 4.1 convolution_convert_fusion.2
  439.3 0.0 reduce-scatter.4.cloned.1.call-update
  439.4 0.1 reshape.127
  439.5 0.8 gather_fusion.4
  440.2 0.1 reshape.128
  440.3 0.6 copy.31
  441.0 151.4 %all-to-all-done.3 = bf16[64,8,3584]{2,1,0:T(8,128)(2,1)} async-done(((bf16[64,8,3584]{2,1,0:T(8,128)(2,1)}), bf16[64,8,3584]{2,1,0:T(8,128)(2,1)}, u32[]{:S(2)}, u32[]{:S(2)}) %all-to-all-start.3) | async-done | bytes 3670048 | tf_op jit(solution)/shard_map/all_to_all | solution.py:88
  592.4 2.6 convert_reduce_fusion
  595.0 0.8 gather_fusion.3
  595.8 0.4 reshape.126
  596.2 1.5 reduce_sum.50
  (18 shorter events, 0.1 us)
Async XLA Ops:
  12.8 33.3 %all-to-all-start = ((bf16[64,1,8]{2,1,0:T(2,128)(2,1)}), bf16[64,1,8]{2,1,0:T(2,128)(2,1)S(1)}, u32[]{:S(2)}, u32[]{:S(2)}) async-start(bf16[64,1,8]{2,1,0:T(2,128)(2,1)} %copy.29), calls=%async_computation | async-start | bytes 65536 | tf_op jit(solution)/shard_map/all_to_all | solution.py:55
  48.2 5.8 copy-start
  48.2 172.1 %all-to-all-start.2 = ((bf16[64,8,3584]{2,1,0:T(8,128)(2,1)}), bf16[64,8,3584]{2,1,0:T(8,128)(2,1)}, u32[]{:S(2)}, u32[]{:S(2)}) async-start(bf16[64,8,3584]{2,1,0:T(8,128)(2,1)} %bitcast.65), calls=%async_computation.2 | async-start | bytes 7340032 | tf_op jit(solution)/shard_map/all_to_all | solution.py:53
  222.4 6.2 %copy-start.1 = (bf16[1,448,128]{2,1,0:T(8,128)(2,1)S(1)}, bf16[1,448,128]{2,1,0:T(8,128)(2,1)}, u32[]{:S(2)}) copy-start(bf16[1,448,128]{2,1,0:T(8,128)(2,1)} %param.11) | copy-start | bytes 344068
  222.4 19.8 %copy-start.2 = (bf16[1,448,128]{2,1,0:T(8,128)(2,1)S(1)}, bf16[1,448,128]{2,1,0:T(8,128)(2,1)}, u32[]{:S(2)}) copy-start(bf16[1,448,128]{2,1,0:T(8,128)(2,1)} %param.12) | copy-start | bytes 344068
  222.4 33.3 %copy-start.3 = (bf16[1,448,128]{2,1,0:T(8,128)(2,1)S(1)}, bf16[1,448,128]{2,1,0:T(8,128)(2,1)}, u32[]{:S(2)}) copy-start(bf16[1,448,128]{2,1,0:T(8,128)(2,1)} %param.13) | copy-start | bytes 344068
  222.4 173.1 %all-to-all-start.1 = ((bf16[64,8,3584]{2,1,0:T(8,128)(2,1)}), bf16[64,8,3584]{2,1,0:T(8,128)(2,1)}, u32[]{:S(2)}, u32[]{:S(2)}) async-start(bf16[64,8,3584]{2,1,0:T(8,128)(2,1)} %bitcast.64), calls=%async_computation.1 | async-start | bytes 7340032 | tf_op jit(solution)/shard_map/all_to_all | solution.py:54
  400.3 20.4 %all-to-all-start.4 = ((bf16[64,1,8]{2,1,0:T(2,128)(2,1)}), bf16[64,1,8]{2,1,0:T(2,128)(2,1)S(1)}, u32[]{:S(2)}, u32[]{:S(2)}) async-start(bf16[64,1,8]{2,1,0:T(2,128)(2,1)} %convert_element_type.125), calls=%async_computation.4 | async-start | bytes 65536 | tf_op jit(solution)/shard_map/all_to_all | solution.py:95
  410.6 15.9 %copy-start.4 = (bf16[512,128]{0,1:T(8,128)(2,1)S(1)}, bf16[512,128]{0,1:T(8,128)(2,1)}, u32[]{:S(2)}) copy-start(bf16[512,128]{0,1:T(8,128)(2,1)} %get-tuple-element.26) | copy-start | bytes 393220
  420.8 171.6 %all-to-all-start.3 = ((bf16[64,8,3584]{2,1,0:T(8,128)(2,1)}), bf16[64,8,3584]{2,1,0:T(8,128)(2,1)}, u32[]{:S(2)}, u32[]{:S(2)}) async-start(bf16[64,8,3584]{2,1,0:T(8,128)(2,1)} %fusion), calls=%async_computation.3 | async-start | bytes 7340032 | tf_op jit(solution)/shard_map/all_to_all | solution.py:88
  426.4 171.3 %reduce-scatter.8.cloned.1.call-start = ((), (), s32[]{:S(2)}) async-start(), calls=%async_computation.10 | async-start | bytes 1032192 | tf_op jit(solution)/shard_map/reduce_scatter | solution.py:119
  430.9 166.9 %reduce-scatter.6.cloned.1.call-start = ((), (), s32[]{:S(2)}) async-start(), calls=%async_computation.9 | async-start | bytes 1032192 | tf_op jit(solution)/shard_map/reduce_scatter | solution.py:116
  435.1 162.7 %reduce-scatter.4.cloned.1.call-start = ((), (), s32[]{:S(2)}) async-start(), calls=%async_computation.8 | async-start | bytes 1032192 | tf_op jit(solution)/shard_map/reduce_scatter | solution.py:113
Sparse Core Ops, SparseCore 0:
  431.0 37.9 reduce-scatter.7
  472.3 39.6 reduce-scatter.5
  515.5 39.6 reduce-scatter.3
where the time goes:
time: 605 us; the launch traced here: 604 us
  waiting for transfers between devices  459 us (76%)
  starting transfers between devices  42.4 us (7%)
  blocking collectives  40.6 us (7%)
  matrix products  27.7 us (5%)
  local copies, waits for them, and re-layouts  14.9 us (2%)
  between operations  14 us (2%)
    all_to_all x1, waiting for transfers between devices, per_device(): lax.all_to_all(spread_tokens, 'ep', split_axis=0, concat_axis=0, tiled=True)  166 us
    all_to_all x1, waiting for transfers between devices, per_device(): lax.all_to_all(token_part.reshape(ep_size, capacity, features), 'ep', spl...  151 us
    all_to_all x1, waiting for transfers between devices, per_device(): lax.all_to_all(spread_grads, 'ep', split_axis=0, concat_axis=0, tiled=True)  119 us
    all_to_all x1, starting transfers between devices, per_device(): lax.all_to_all(spread_probs.astype(jnp.bfloat16), 'ep', split_axis=0, con...  18.7 us
    all_gather x1, blocking collectives, per_device(): lax.all_gather(gate_weight, 'dp', axis=1, tiled=True)  13.6 us
    all_gather x1, blocking collectives, per_device(): lax.all_gather(up_weight, 'dp', axis=1, tiled=True)  13.5 us
    all_gather x1, blocking collectives, per_device(): lax.all_gather(down_weight, 'dp', axis=1, tiled=True)  13.5 us
    all_to_all x1, waiting for transfers between devices, per_device(): lax.all_to_all(spread_probs.astype(jnp.bfloat16), 'ep', split_axis=0, con...  12.8 us
  transfers between devices with their start and end apart: 8, of which 5 were waited for; matrix products, arithmetic and copies ran while one was open for 6% of the time, Pallas kernels for 0%

commit v1 on v0

--- a/solution.py
+++ b/solution.py
@@ -59,9 +59,15 @@
     rows_in = rows_tok.reshape(-1, features)
     rows_grad = rows_grd.reshape(-1, features)
     rows_prob = rows_prb.reshape(-1)
+
+    def update_corner(u):
+        all_rows = jnp.stack(lax.axis_size("dp") * [u], axis=0)
+        opened = jnp.concatenate(lax.all_to_all(all_rows, "dp", 0, 0), axis=1)
+        return opened
+
     gate_all, up_all, down_all = (
         lax.all_gather(gate_weight, "dp", axis=1, tiled=True),
-        lax.all_gather(up_weight, "dp", axis=1, tiled=True),
+        update_corner(up_weight),
         lax.all_gather(down_weight, "dp", axis=1, tiled=True),
     )
     gate_full = gate_all[0]

time: 605 us -> 626 us (1.035)
  the two profiles are of different devices: /device:TPU:2 before, /device:TPU:8 now
where the time goes in v1:
time: 626 us
  waiting for transfers between devices  474 us (76%)
  blocking collectives  59.5 us (10%)
  starting transfers between devices  29.3 us (5%)
  matrix products  27.8 us (4%)
  local copies, waits for them, and re-layouts  15.4 us (2%)
  between operations  14 us (2%)
    all_to_all x1, waiting for transfers between devices, per_device(): lax.all_to_all(spread_tokens, 'ep', split_axis=0, concat_axis=0, tiled=True)  167 us
    all_to_all x1, waiting for transfers between devices, per_device(): lax.all_to_all(token_part.reshape(ep_size, capacity, features), 'ep', spl...  151 us
    all_to_all x1, waiting for transfers between devices, per_device(): lax.all_to_all(spread_grads, 'ep', split_axis=0, concat_axis=0, tiled=True)  133 us
    all_to_all x1, blocking collectives, per_device(): lax.all_to_all(spread_probs.astype(jnp.bfloat16), 'ep', split_axis=0, con...  32.3 us
    all_to_all x1, waiting for transfers between devices, update_corner(): opened = jnp.concatenate(lax.all_to_all(all_rows, 'dp', 0, 0), axis=1)  13.7 us
    all_gather x1, blocking collectives, per_device(): lax.all_gather(gate_weight, 'dp', axis=1, tiled=True)  13.6 us
    all_gather x1, blocking collectives, per_device(): lax.all_gather(down_weight, 'dp', axis=1, tiled=True)  13.5 us
  transfers between devices with their start and end apart: 8, of which 5 were waited for; matrix products, arithmetic and copies ran while one was open for 5% of the time, Pallas kernels for 0%

profile of v1, /device:TPU:8, one launch (start us, length us, event | category | flops | bytes accessed | tf_op | source)
XLA Modules:
  0.0 625.6 jit_solution(13486019773526643766)
XLA Ops:
  7.2 0.0 copy-start.1
  7.2 0.7 broadcast_multiply_fusion
  7.9 0.8 copy.27
  8.7 0.8 copy.25
  9.4 0.1 reshape.122
  9.5 0.1 copy.26
  9.6 0.1 mul.61
  9.7 0.1 eq.15
  9.8 0.1 fusion.16
  9.9 0.1 reduce_window_sum.11
  10.0 0.2 select_reduce_fusion
  10.2 0.7 scatter_custom_fusion
  10.9 0.1 pad_maximum_fusion
  11.0 0.8 gather_fusion
  11.8 0.1 convert_element_type.101
  11.9 0.1 copy.28
  12.0 0.1 broadcast_in_dim.45
  12.0 0.1 convert_element_type.102
  12.1 0.1 copy.29
  12.2 32.3 %all_to_all.32 = bf16[64,1,8]{2,1,0:T(2,128)(2,1)S(1)} all-to-all(bf16[64,1,8]{2,1,0:T(2,128)(2,1)S(1)} %copy.29), channel_id=1, replica_groups=mesh['ep'=64,'dp'=8] {'ep'}, dimensions={0} | all-to-all | bytes 2048 | tf_op jit(solution)/shard_map/all_to_all | solution.py:55
  44.6 1.9 stack.2
  46.5 4.3 all-to-all-start.3
  50.8 0.0 copy-done.1
  50.9 0.8 gather_fusion.2
  51.7 13.7 %all-to-all-done.3 = bf16[8,1,448,128]{3,2,1,0:T(8,128)(2,1)S(1)} async-done(((bf16[8,1,448,128]{3,2,1,0:T(8,128)(2,1)}), bf16[8,1,448,128]{3,2,1,0:T(8,128)(2,1)S(1)}, u32[]{:S(2)}, u32[]{:S(2)}) %all-to-all-start.3) | async-done | bytes 917536 | tf_op jit(solution)/shard_map/all_to_all | solution.py:65
  65.4 2.1 broadcast_in_dim.51
  67.5 6.4 %all-to-all-start.2 = ((bf16[64,8,3584]{2,1,0:T(8,128)(2,1)}), bf16[64,8,3584]{2,1,0:T(8,128)(2,1)}, u32[]{:S(2)}, u32[]{:S(2)}) async-start(bf16[64,8,3584]{2,1,0:T(8,128)(2,1)} %bitcast.64), calls=%async_computation.2 | async-start | bytes 7340032 | tf_op jit(solution)/shard_map/all_to_all | solution.py:53
  73.8 0.0 copy-done.2
  73.9 0.8 gather_fusion.1
  74.7 166.7 %all-to-all-done.2 = bf16[64,8,3584]{2,1,0:T(8,128)(2,1)} async-done(((bf16[64,8,3584]{2,1,0:T(8,128)(2,1)}), bf16[64,8,3584]{2,1,0:T(8,128)(2,1)}, u32[]{:S(2)}, u32[]{:S(2)}) %all-to-all-start.2) | async-done | bytes 3670048 | tf_op jit(solution)/shard_map/all_to_all | solution.py:53
  241.4 2.2 broadcast_in_dim.49
  243.6 6.2 all-to-all-start.1
  249.8 13.6 %all_gather.7 = bf16[1,3584,128]{2,1,0:T(8,128)(2,1)S(1)} all-gather(bf16[1,448,128]{2,1,0:T(8,128)(2,1)S(1)} %copy-done.3), channel_id=1, replica_groups=mesh['ep'=64,'dp'=8] {'dp'}, dimensions={1}, use_global_device_ids=true | all-gather | bytes 1032192 | tf_op jit(solution)/shard_map/all_gather | solution.py:69
  263.5 13.5 %all_gather.6 = bf16[1,3584,128]{2,1,0:T(8,128)(2,1)S(1)} all-gather(bf16[1,448,128]{2,1,0:T(8,128)(2,1)S(1)} %copy-done.4), channel_id=1, replica_groups=mesh['ep'=64,'dp'=8] {'dp'}, dimensions={1}, use_global_device_ids=true | all-gather | bytes 1032192 | tf_op jit(solution)/shard_map/all_gather | solution.py:71
  277.0 0.1 convert_reduce_fusion.1
  277.1 0.1 reshape.132
  277.2 3.4 fusion.3
  280.5 3.4 fusion.5
  283.9 132.8 %all-to-all-done.1 = bf16[64,8,3584]{2,1,0:T(8,128)(2,1)} async-done(((bf16[64,8,3584]{2,1,0:T(8,128)(2,1)}), bf16[64,8,3584]{2,1,0:T(8,128)(2,1)}, u32[]{:S(2)}, u32[]{:S(2)}) %all-to-all-start.1) | async-done | bytes 3670048 | tf_op jit(solution)/shard_map/all_to_all | solution.py:54
  416.8 4.1 multiply_reduce_fusion
  420.9 0.7 convert_element_type.125
  421.6 6.0 all-to-all-start.5
  427.6 1.1 fusion.11
  428.8 3.1 fusion
  431.9 9.5 %all-to-all-done.5 = bf16[64,1,8]{2,1,0:T(2,128)(2,1)S(1)} async-done(((bf16[64,1,8]{2,1,0:T(2,128)(2,1)}), bf16[64,1,8]{2,1,0:T(2,128)(2,1)S(1)}, u32[]{:S(2)}, u32[]{:S(2)}) %all-to-all-start.5) | async-done | bytes 1056 | tf_op jit(solution)/shard_map/all_to_all | solution.py:101
  441.3 6.3 %all-to-all-start.4 = ((bf16[64,8,3584]{2,1,0:T(8,128)(2,1)}), bf16[64,8,3584]{2,1,0:T(8,128)(2,1)}, u32[]{:S(2)}, u32[]{:S(2)}) async-start(bf16[64,8,3584]{2,1,0:T(8,128)(2,1)} %fusion), calls=%async_computation.4 | async-start | bytes 7340032 | tf_op jit(solution)/shard_map/all_to_all | solution.py:94
  447.6 0.0 reduce-scatter.8.cloned.1.call-start
  447.7 4.4 convolution_convert_fusion
  452.1 0.0 reduce-scatter.8.cloned.1.call-update
  452.1 0.0 reduce-scatter.6.cloned.1.call-start
  452.1 4.1 convolution_convert_fusion.1
  456.3 0.0 reduce-scatter.6.cloned.1.call-update
  456.3 0.0 reduce-scatter.4.cloned.1.call-start
  456.3 4.1 convolution_convert_fusion.2
  460.5 0.0 reduce-scatter.4.cloned.1.call-update
  460.6 0.1 reshape.130
  460.7 0.8 gather_fusion.4
  461.4 0.1 reshape.131
  461.5 0.6 copy.31
  462.2 151.5 %all-to-all-done.4 = bf16[64,8,3584]{2,1,0:T(8,128)(2,1)} async-done(((bf16[64,8,3584]{2,1,0:T(8,128)(2,1)}), bf16[64,8,3584]{2,1,0:T(8,128)(2,1)}, u32[]{:S(2)}, u32[]{:S(2)}) %all-to-all-start.4) | async-done | bytes 3670048 | tf_op jit(solution)/shard_map/all_to_all | solution.py:94
  613.7 2.6 convert_reduce_fusion
  616.3 0.8 gather_fusion.3
  617.1 0.4 reshape.129
  617.5 1.5 reduce_sum.50
  (21 shorter events, 0.1 us)
Async XLA Ops:
  7.2 43.7 %copy-start.1 = (bf16[24,3584]{1,0:T(8,128)(2,1)S(1)}, bf16[24,3584]{1,0:T(8,128)(2,1)}, u32[]{:S(2)}) copy-start(bf16[24,3584]{1,0:T(8,128)(2,1)} %param.7) | copy-start | bytes 516100
  46.5 18.8 %all-to-all-start.3 = ((bf16[8,1,448,128]{3,2,1,0:T(8,128)(2,1)}), bf16[8,1,448,128]{3,2,1,0:T(8,128)(2,1)S(1)}, u32[]{:S(2)}, u32[]{:S(2)}) async-start(bf16[8,1,448,128]{3,2,1,0:T(8,128)(2,1)} %stack.2), calls=%async_computation.3 | async-start | bytes 1835008 | tf_op jit(solution)/shard_map/all_to_all | solution.py:65
  67.5 6.4 %copy-start.2 = (bf16[24,3584]{1,0:T(8,128)(2,1)S(1)}, bf16[24,3584]{1,0:T(8,128)(2,1)}, u32[]{:S(2)}) copy-start(bf16[24,3584]{1,0:T(8,128)(2,1)} %param.8) | copy-start | bytes 516100
  67.5 174.0 %all-to-all-start.2 = ((bf16[64,8,3584]{2,1,0:T(8,128)(2,1)}), bf16[64,8,3584]{2,1,0:T(8,128)(2,1)}, u32[]{:S(2)}, u32[]{:S(2)}) async-start(bf16[64,8,3584]{2,1,0:T(8,128)(2,1)} %bitcast.64), calls=%async_computation.2 | async-start | bytes 7340032 | tf_op jit(solution)/shard_map/all_to_all | solution.py:53
  243.6 6.3 %copy-start.3 = (bf16[1,448,128]{2,1,0:T(8,128)(2,1)S(1)}, bf16[1,448,128]{2,1,0:T(8,128)(2,1)}, u32[]{:S(2)}) copy-start(bf16[1,448,128]{2,1,0:T(8,128)(2,1)} %param.11) | copy-start | bytes 344068
  243.6 19.9 %copy-start.4 = (bf16[1,448,128]{2,1,0:T(8,128)(2,1)S(1)}, bf16[1,448,128]{2,1,0:T(8,128)(2,1)}, u32[]{:S(2)}) copy-start(bf16[1,448,128]{2,1,0:T(8,128)(2,1)} %param.13) | copy-start | bytes 344068
  243.6 173.2 %all-to-all-start.1 = ((bf16[64,8,3584]{2,1,0:T(8,128)(2,1)}), bf16[64,8,3584]{2,1,0:T(8,128)(2,1)}, u32[]{:S(2)}, u32[]{:S(2)}) async-start(bf16[64,8,3584]{2,1,0:T(8,128)(2,1)} %bitcast.63), calls=%async_computation.1 | async-start | bytes 7340032 | tf_op jit(solution)/shard_map/all_to_all | solution.py:54
  421.6 19.7 %all-to-all-start.5 = ((bf16[64,1,8]{2,1,0:T(2,128)(2,1)}), bf16[64,1,8]{2,1,0:T(2,128)(2,1)S(1)}, u32[]{:S(2)}, u32[]{:S(2)}) async-start(bf16[64,1,8]{2,1,0:T(2,128)(2,1)} %convert_element_type.125), calls=%async_computation.5 | async-start | bytes 65536 | tf_op jit(solution)/shard_map/all_to_all | solution.py:101
  427.6 1.2 copy-start
  431.9 15.8 %copy-start.5 = (bf16[512,128]{0,1:T(8,128)(2,1)S(1)}, bf16[512,128]{0,1:T(8,128)(2,1)}, u32[]{:S(2)}) copy-start(bf16[512,128]{0,1:T(8,128)(2,1)} %get-tuple-element.26) | copy-start | bytes 393220
  441.3 172.3 %all-to-all-start.4 = ((bf16[64,8,3584]{2,1,0:T(8,128)(2,1)}), bf16[64,8,3584]{2,1,0:T(8,128)(2,1)}, u32[]{:S(2)}, u32[]{:S(2)}) async-start(bf16[64,8,3584]{2,1,0:T(8,128)(2,1)} %fusion), calls=%async_computation.4 | async-start | bytes 7340032 | tf_op jit(solution)/shard_map/all_to_all | solution.py:94
  447.6 171.4 %reduce-scatter.8.cloned.1.call-start = ((), (), s32[]{:S(2)}) async-start(), calls=%async_computation.11 | async-start | bytes 1032192 | tf_op jit(solution)/shard_map/reduce_scatter | solution.py:125
  452.1 167.0 %reduce-scatter.6.cloned.1.call-start = ((), (), s32[]{:S(2)}) async-start(), calls=%async_computation.10 | async-start | bytes 1032192 | tf_op jit(solution)/shard_map/reduce_scatter | solution.py:122
  456.3 162.7 %reduce-scatter.4.cloned.1.call-start = ((), (), s32[]{:S(2)}) async-start(), calls=%async_computation.9 | async-start | bytes 1032192 | tf_op jit(solution)/shard_map/reduce_scatter | solution.py:119
Sparse Core Ops, SparseCore 0:
  452.2 39.4 reduce-scatter.7
  495.1 39.5 reduce-scatter.5
  538.1 39.6 reduce-scatter.3
